TPU v7x, 32 devices: a whole 2x2x4 slice. The times are simulated.
32 devices in a mesh: gx: 4 (over x, core), gy: 8 (over z, y).
Axes of the slice: x: 2, y: 2, z: 4, core: 2. Of those that a mesh axis runs over, the one named last changes fastest.
Arguments:
- activation: bfloat16 [32, 16, 32, 128], P(None, 'gx', 'gy'), may hold values from -6 to 6
- out_grad: bfloat16 [32, 16, 32, 128], P(None, 'gx', 'gy'), may hold values from -6 to 6
- kernel: bfloat16 [3, 3, 3, 32, 32], replicated, may hold values from -0.21875 to 0.21875
Outputs:
- grad_input: bfloat16 [32, 16, 32, 128], P(None, 'gx', 'gy')
- grad_kernel: float32 [3, 3, 3, 32, 32], replicated
All inputs are finite; a program needn't handle non-finite values.
Results may differ from a plain program's by a relative error of at most 0.001.
Values may be sent and summed in bfloat16 or wider, within the bound.
No kernel may reach another device: no remote copies, remote signals or barrier semaphores. Data moves between devices by JAX's collectives and lax.ppermute only.
A program may use at most 64 MiB of HBM per device.

v0:
```python
import jax
import jax.numpy as jnp
from jax import lax
from jax.sharding import PartitionSpec as P


def extended(cells, sides, width):
    for axis, dim in sides:
        count = lax.axis_size(axis)
        ends = count - 1
        head = lax.slice_in_dim(cells, 0, width, axis=dim)
        tail = lax.slice_in_dim(cells, cells.shape[dim] - width, cells.shape[dim], axis=dim)
        cells = jnp.concatenate(
            [
                lax.ppermute(tail, axis, [(i, (i + 1) % count) for i in range(ends)]),
                cells,
                lax.ppermute(head, axis, [((i + 1) % count, i) for i in range(ends)]),
            ],
            axis=dim,
        )
    return cells


def padded_z(block):
    return jnp.pad(block, ((0, 0), (0, 0), (0, 0), (1, 1)))


def contract_cells(left, right):
    return lax.dot_general(
        left, right, (((1,), (1,)), ((), ())), preferred_element_type=jnp.float32
    )


def shards(activation, out_grad, kernel):
    channels = activation.shape[0]
    size_x, size_y, size_z = (activation.shape[1], activation.shape[2], activation.shape[3])
    cell_count = size_x * size_y * size_z
    grad_pad = padded_z(extended(out_grad, (("gx", 1), ("gy", 2)), 1))
    flat_act = activation.reshape(channels, cell_count)
    accumulated = jnp.zeros((channels, cell_count), jnp.float32)
    products = []
    for off_x in range(3):
        for off_y in range(3):
            for off_z in range(3):
                window = grad_pad[
                    :,
                    2 - off_x : 2 - off_x + size_x,
                    2 - off_y : 2 - off_y + size_y,
                    2 - off_z : 2 - off_z + size_z,
                ].reshape(channels, cell_count)
                accumulated = accumulated + jnp.dot(
                    kernel[off_x, off_y, off_z].T, window, preferred_element_type=jnp.float32
                )
                products.append(contract_cells(window, flat_act))
    grad_input = accumulated.reshape(channels, size_x, size_y, size_z).astype(jnp.bfloat16)
    local_terms = jnp.stack(products).reshape(3, 3, 3, channels, channels)
    summed = lax.psum(local_terms, ("gx", "gy"))
    total_cells = size_x * lax.axis_size("gx") * size_y * lax.axis_size("gy") * size_z
    grad_kernel = summed / jnp.sqrt(jnp.float32(total_cells))
    return (grad_input, grad_kernel)


def solution(mesh):
    return jax.shard_map(
        shards,
        mesh=mesh,
        in_specs=(P(None, "gx", "gy", None), P(None, "gx", "gy", None), P()),
        out_specs=(P(None, "gx", "gy", None), P()),
        check_vma=False,
    )
```

profile of v0, /device:TPU:8, one launch (start us, length us, event | category | flops | bytes accessed | tf_op | source)
XLA Modules:
  0.0 171.7 jit_solution(9164996284599008277)
XLA Ops:
  8.1 1.7 %collective-permute-start = (bf16[32,1,4,128]{3,0,2,1:T(8,128)(2,1)S(1)}, bf16[32,1,4,128]{3,0,2,1:T(8,128)(2,1)S(1)}, u32[]{:S(2)}, u32[]{:S(2)}) collective-permute-start(bf16[32,1,4,128]{3,0,2,1:T(8,128)(2,1)S(1)} %copy.183), channel_id=1, source_target_pairs={{0,8},{8,16},{16,24},{1,9},{9,17},{17,25},{2,10},{10,18},{18,26},{... | collective-permute-start | bytes 98312 | tf_op jit(solution)/shard_map/ppermute | solution.py:15
  9.9 1.3 collective-permute-start.1
  11.2 1.6 reshape.104
  12.9 1.3 collective-permute-done.1
  14.3 3.4 %collective-permute-start.2 = (bf16[32,6,1,128]{3,0,2,1:T(8,128)(2,1)S(1)}, bf16[32,6,1,128]{3,0,2,1:T(8,128)(2,1)S(1)}, u32[]{:S(2)}, u32[]{:S(2)}) collective-permute-start(bf16[32,6,1,128]{3,0,2,1:T(8,128)(2,1)S(1)} %get-tuple-element.29), channel_id=1, source_target_pairs={{0,1},{1,2},{2,3},{3,4},{4,5},{5,6},{6,7},{8,9},{9,10},{10,11},{11... | collective-permute-start | bytes 147464 | tf_op jit(solution)/shard_map/ppermute | solution.py:15
  17.7 3.3 %collective-permute-start.3 = (bf16[32,6,1,128]{3,0,2,1:T(8,128)(2,1)S(1)}, bf16[32,6,1,128]{3,0,2,1:T(8,128)(2,1)S(1)}, u32[]{:S(2)}, u32[]{:S(2)}) collective-permute-start(bf16[32,6,1,128]{3,0,2,1:T(8,128)(2,1)S(1)} %get-tuple-element.30), channel_id=1, source_target_pairs={{1,0},{2,1},{3,2},{4,3},{5,4},{6,5},{7,6},{9,8},{10,9},{11,10},{12... | collective-permute-start | bytes 147464 | tf_op jit(solution)/shard_map/ppermute | solution.py:17
  24.0 1.3 fusion.161
  53.3 1.1 convolution_bitcast_fusion.10
  55.2 1.0 reshape.110
  57.1 1.2 convolution_add_fusion.12
  58.3 1.0 convolution_add_fusion.11
  59.3 1.0 convolution_add_fusion.10
  60.3 1.0 convolution_add_fusion.9
  61.3 1.0 convolution_add_fusion.8
  62.3 1.0 convolution_add_fusion.7
  63.3 1.0 convolution_add_fusion.6
  64.3 1.0 convolution_add_fusion.5
  65.2 1.0 convolution_add_fusion.4
  66.2 1.0 convolution_add_fusion.3
  67.2 1.0 convolution_add_fusion.2
  68.2 1.0 fusion.13
  70.1 1.0 fusion.14
  71.9 91.1 %all-reduce.3.cloned.1.call-done = f32[3,3,3,32,32]{4,3,2,1,0:T(8,128)} async-done(((f32[3,3,3,32,32]{4,3,2,1,0:T(8,128)}), f32[3,3,3,32,32]{4,3,2,1,0:T(8,128)}) %all-reduce.3.cloned.1.call-update) | async-done | bytes 110608 | tf_op jit(solution)/shard_map/psum | solution.py:57
  163.0 1.8 %broadcast_multiply_fusion = f32[3,3,3,32,32]{4,3,2,1,0:T(8,128)} fusion(f32[3,3,3,32,32]{4,3,2,1,0:T(8,128)} %all-reduce.3.cloned.1.call-done), kind=kLoop, calls=%fused_computation.117 | loop fusion | flops 27648 | bytes 221184 | tf_op jit(solution)/shard_map/div | solution.py:59
  (150 shorter events, 35.1 us)
Async XLA Ops:
  7.2 18.1 %copy-start = (bf16[32,4,4,128]{3,2,1,0:T(4,128)(2,1)S(1)}, bf16[32,4,4,128]{3,2,1,0:T(4,128)(2,1)}, u32[]{:S(2)}) copy-start(bf16[32,4,4,128]{3,2,1,0:T(4,128)(2,1)} %param.3) | copy-start | bytes 393220
  7.2 5.6 %copy-start.1 = (bf16[32,4,4,128]{3,2,1,0:T(4,128)(2,1)S(1)}, bf16[32,4,4,128]{3,2,1,0:T(4,128)(2,1)}, u32[]{:S(2)}) copy-start(bf16[32,4,4,128]{3,2,1,0:T(4,128)(2,1)} %param.4) | copy-start | bytes 393220
  7.2 155.8 %all-reduce.3.cloned.1.call-start = ((), (), s32[]{:S(2)}) async-start(), calls=%async_computation | async-start | bytes 884736 | tf_op jit(solution)/shard_map/psum | solution.py:57
  8.1 4.7 %collective-permute-start = (bf16[32,1,4,128]{3,0,2,1:T(8,128)(2,1)S(1)}, bf16[32,1,4,128]{3,0,2,1:T(8,128)(2,1)S(1)}, u32[]{:S(2)}, u32[]{:S(2)}) collective-permute-start(bf16[32,1,4,128]{3,0,2,1:T(8,128)(2,1)S(1)} %copy.183), channel_id=1, source_target_pairs={{0,8},{8,16},{16,24},{1,9},{9,17},{17,25},{2,10},{10,18},{18,26},{... | collective-permute-start | bytes 98312 | tf_op jit(solution)/shard_map/ppermute | solution.py:15
  9.9 4.4 %collective-permute-start.1 = (bf16[32,1,4,128]{3,0,2,1:T(8,128)(2,1)S(1)}, bf16[32,1,4,128]{3,0,2,1:T(8,128)(2,1)S(1)}, u32[]{:S(2)}, u32[]{:S(2)}) collective-permute-start(bf16[32,1,4,128]{3,0,2,1:T(8,128)(2,1)S(1)} %copy.184), channel_id=1, source_target_pairs={{8,0},{16,8},{24,16},{9,1},{17,9},{25,17},{10,2},{18,10},{26,18},{... | collective-permute-start | bytes 98312 | tf_op jit(solution)/shard_map/ppermute | solution.py:17
  14.3 8.7 %collective-permute-start.2 = (bf16[32,6,1,128]{3,0,2,1:T(8,128)(2,1)S(1)}, bf16[32,6,1,128]{3,0,2,1:T(8,128)(2,1)S(1)}, u32[]{:S(2)}, u32[]{:S(2)}) collective-permute-start(bf16[32,6,1,128]{3,0,2,1:T(8,128)(2,1)S(1)} %get-tuple-element.29), channel_id=1, source_target_pairs={{0,1},{1,2},{2,3},{3,4},{4,5},{5,6},{6,7},{8,9},{9,10},{10,11},{11... | collective-permute-start | bytes 147464 | tf_op jit(solution)/shard_map/ppermute | solution.py:15
  17.7 6.0 %collective-permute-start.3 = (bf16[32,6,1,128]{3,0,2,1:T(8,128)(2,1)S(1)}, bf16[32,6,1,128]{3,0,2,1:T(8,128)(2,1)S(1)}, u32[]{:S(2)}, u32[]{:S(2)}) collective-permute-start(bf16[32,6,1,128]{3,0,2,1:T(8,128)(2,1)S(1)} %get-tuple-element.30), channel_id=1, source_target_pairs={{1,0},{2,1},{3,2},{4,3},{5,4},{6,5},{7,6},{9,8},{10,9},{11,10},{12... | collective-permute-start | bytes 147464 | tf_op jit(solution)/shard_map/ppermute | solution.py:17
  33.2 1.6 copy-start.3
  35.6 1.6 copy-start.7
  49.6 1.8 %copy-start.4 = (bf16[32,4,4,128]{3,0,2,1:T(8,128)(2,1)S(1)}, bf16[32,4,4,128]{3,0,2,1:T(8,128)(2,1)}, u32[]{:S(2)}) copy-start(bf16[32,4,4,128]{3,0,2,1:T(8,128)(2,1)} %get-tuple-element.26) | copy-start | bytes 393220
  50.7 1.8 %copy-start.2 = (bf16[32,4,4,128]{3,0,2,1:T(8,128)(2,1)S(1)}, bf16[32,4,4,128]{3,0,2,1:T(8,128)(2,1)}, u32[]{:S(2)}) copy-start(bf16[32,4,4,128]{3,0,2,1:T(8,128)(2,1)} %get-tuple-element.27) | copy-start | bytes 393220
  56.2 2.2 %copy-start.11 = (bf16[32,2048]{1,0:T(8,128)(2,1)S(1)}, bf16[32,2048]{1,0:T(8,128)(2,1)}, u32[]{:S(2)}) copy-start(bf16[32,2048]{1,0:T(8,128)(2,1)} %reshape.93) | copy-start | bytes 393220
  57.1 2.2 %copy-start.13 = (bf16[32,2048]{1,0:T(8,128)(2,1)S(1)}, bf16[32,2048]{1,0:T(8,128)(2,1)}, u32[]{:S(2)}) copy-start(bf16[32,2048]{1,0:T(8,128)(2,1)} %reshape.94) | copy-start | bytes 393220
  58.3 2.0 %copy-start.9 = (bf16[32,2048]{1,0:T(8,128)(2,1)S(1)}, bf16[32,2048]{1,0:T(8,128)(2,1)}, u32[]{:S(2)}) copy-start(bf16[32,2048]{1,0:T(8,128)(2,1)} %reshape.95) | copy-start | bytes 393220
  59.3 2.0 %copy-start.10 = (bf16[32,2048]{1,0:T(8,128)(2,1)S(1)}, bf16[32,2048]{1,0:T(8,128)(2,1)}, u32[]{:S(2)}) copy-start(bf16[32,2048]{1,0:T(8,128)(2,1)} %reshape.96) | copy-start | bytes 393220
  60.3 2.0 %copy-start.12 = (bf16[32,2048]{1,0:T(8,128)(2,1)S(1)}, bf16[32,2048]{1,0:T(8,128)(2,1)}, u32[]{:S(2)}) copy-start(bf16[32,2048]{1,0:T(8,128)(2,1)} %reshape.97) | copy-start | bytes 393220
  61.3 2.0 %copy-start.14 = (bf16[32,2048]{1,0:T(8,128)(2,1)S(1)}, bf16[32,2048]{1,0:T(8,128)(2,1)}, u32[]{:S(2)}) copy-start(bf16[32,2048]{1,0:T(8,128)(2,1)} %reshape.98) | copy-start | bytes 393220
  62.3 2.0 %copy-start.15 = (bf16[32,2048]{1,0:T(8,128)(2,1)S(1)}, bf16[32,2048]{1,0:T(8,128)(2,1)}, u32[]{:S(2)}) copy-start(bf16[32,2048]{1,0:T(8,128)(2,1)} %reshape.99) | copy-start | bytes 393220
  63.3 2.0 %copy-start.16 = (bf16[32,2048]{1,0:T(8,128)(2,1)S(1)}, bf16[32,2048]{1,0:T(8,128)(2,1)}, u32[]{:S(2)}) copy-start(bf16[32,2048]{1,0:T(8,128)(2,1)} %reshape.100) | copy-start | bytes 393220
  64.2 2.0 %copy-start.17 = (bf16[32,2048]{1,0:T(8,128)(2,1)S(1)}, bf16[32,2048]{1,0:T(8,128)(2,1)}, u32[]{:S(2)}) copy-start(bf16[32,2048]{1,0:T(8,128)(2,1)} %reshape.101) | copy-start | bytes 393220
  65.2 2.0 %copy-start.18 = (bf16[32,2048]{1,0:T(8,128)(2,1)S(1)}, bf16[32,2048]{1,0:T(8,128)(2,1)}, u32[]{:S(2)}) copy-start(bf16[32,2048]{1,0:T(8,128)(2,1)} %reshape.102) | copy-start | bytes 393220
  66.2 2.0 %copy-start.19 = (bf16[32,2048]{1,0:T(8,128)(2,1)S(1)}, bf16[32,2048]{1,0:T(8,128)(2,1)}, u32[]{:S(2)}) copy-start(bf16[32,2048]{1,0:T(8,128)(2,1)} %reshape.103) | copy-start | bytes 393220
  67.2 2.0 %copy-start.8 = (bf16[32,2048]{1,0:T(8,128)(2,1)S(1)}, bf16[32,2048]{1,0:T(8,128)(2,1)}, u32[]{:S(2)}) copy-start(bf16[32,2048]{1,0:T(8,128)(2,1)} %reshape.104) | copy-start | bytes 393220
  68.2 1.9 %copy-start.6 = (bf16[32,2048]{1,0:T(8,128)(2,1)S(1)}, bf16[32,2048]{1,0:T(8,128)(2,1)}, u32[]{:S(2)}) copy-start(bf16[32,2048]{1,0:T(8,128)(2,1)} %reshape.105) | copy-start | bytes 393220
  (2 other events, 2.4 us)
Sparse Core Ops, SparseCore 0:
  31.4 131.5 all-reduce.2
where the time goes:
time: 173 us; the launch traced here: 172 us
  waiting for transfers between devices  93.2 us (54%)
  matrix products  31 us (18%)
  local copies, waits for them, and re-layouts  19.9 us (12%)
  between operations  14.8 us (9%)
  starting transfers between devices  9.81 us (6%)
  other arithmetic  2.88 us (2%)
    psum x1, waiting for transfers between devices, shards(): summed = lax.psum(local_terms, ('gx', 'gy'))  91.1 us
    dot_general x27, matrix products, shards(): jnp.dot(kernel[off_x, off_y, off_z].T, window, preferred_element_type=jnp...  25.8 us
    reshape x27, local copies, waits for them, and re-layouts, shards(): window = grad_pad[:, 2 - off_x:2 - off_x + size_x, 2 - off_y:2 - off_y +...  13.6 us
    dot_general x27, matrix products, contract_cells(): lax.dot_general(left, right, (((1,), (1,)), ((), ())), preferred_element_...  5.22 us
    ppermute x2, starting transfers between devices, extended(): lax.ppermute(tail, axis, [(i, (i + 1) % count) for i in range(ends)])  5.17 us
    ppermute x2, starting transfers between devices, extended(): lax.ppermute(head, axis, [((i + 1) % count, i) for i in range(ends)])  4.61 us
    slice x29, local copies, waits for them, and re-layouts, shards(): grad_pad[:, 2 - off_x:2 - off_x + size_x, 2 - off_y:2 - off_y + size_y, 2...  3.73 us
  transfers between devices with their start and end apart: 5, of which 3 were waited for; matrix products, arithmetic and copies ran while one was open for 25% of the time, Pallas kernels for 0%

commit v1 on v0

--- a/solution.py
+++ b/solution.py
@@ -54,7 +54,7 @@
                 products.append(contract_cells(window, flat_act))
     grad_input = accumulated.reshape(channels, size_x, size_y, size_z).astype(jnp.bfloat16)
     local_terms = jnp.stack(products).reshape(3, 3, 3, channels, channels)
-    summed = lax.psum(local_terms, ("gx", "gy"))
+    summed = jnp.sum(lax.all_gather(local_terms, ("gx", "gy")), axis=0)
     total_cells = size_x * lax.axis_size("gx") * size_y * lax.axis_size("gy") * size_z
     grad_kernel = summed / jnp.sqrt(jnp.float32(total_cells))
     return (grad_input, grad_kernel)

time: 173 us -> 151 us (0.87)
  matrix products: 31 us -> 14.2 us
  waiting for transfers between devices: 93.2 us -> 76.7 us
  other arithmetic: 2.88 us -> 9.62 us
  local copies, waits for them, and re-layouts: 19.9 us -> 24.6 us
    psum x1 -> x0, waiting for transfers between devices: 91.1 us -> none  [shards(): summed = lax.psum(local_terms, ('gx', 'gy'))]
    all_gather x0 -> x1, waiting for transfers between devices: none -> 72.1 us  [shards(): summed = jnp.sum(lax.all_gather(local_terms, ('gx', 'gy')), axis=0)]
    dot_general x27, matrix products: 25.8 us -> 8.94 us  [shards(): jnp.dot(kernel[off_x, off_y, off_z].T, window, preferred_element_type=jnp...]
    reduce_sum x0 -> x1, other arithmetic: none -> 6.85 us  [shards(): summed = jnp.sum(lax.all_gather(local_terms, ('gx', 'gy')), axis=0)]
    slice x29, local copies, waits for them, and re-layouts: 3.73 us -> 9.21 us  [shards(): grad_pad[:, 2 - off_x:2 - off_x + size_x, 2 - off_y:2 - off_y + size_y, 2...]
    ppermute x2, waiting for transfers between devices: 0.01 us -> 2.62 us  [extended(): lax.ppermute(tail, axis, [(i, (i + 1) % count) for i in range(ends)])]
  transfers between devices with their start and end apart: 5 -> 5, of which waited for: 3 -> 3; matrix products, arithmetic and copies ran while one was open for 25% -> 23% of each run, Pallas kernels for 0% -> 0%
where the time goes in v1:
time: 151 us; the launch traced here: 149 us
  waiting for transfers between devices  76.7 us (51%)
  local copies, waits for them, and re-layouts  24.6 us (16%)
  between operations  14.7 us (10%)
  matrix products  14.2 us (9%)
  other arithmetic  9.62 us (6%)
  starting transfers between devices  8.91 us (6%)
    all_gather x1, waiting for transfers between devices, shards(): summed = jnp.sum(lax.all_gather(local_terms, ('gx', 'gy')), axis=0)  72.1 us
    reshape x27, local copies, waits for them, and re-layouts, shards(): window = grad_pad[:, 2 - off_x:2 - off_x + size_x, 2 - off_y:2 - off_y +...  11.9 us
    slice x29, local copies, waits for them, and re-layouts, shards(): grad_pad[:, 2 - off_x:2 - off_x + size_x, 2 - off_y:2 - off_y + size_y, 2...  9.21 us
    dot_general x27, matrix products, shards(): jnp.dot(kernel[off_x, off_y, off_z].T, window, preferred_element_type=jnp...  8.94 us
    reduce_sum x1, other arithmetic, shards(): summed = jnp.sum(lax.all_gather(local_terms, ('gx', 'gy')), axis=0)  6.85 us
    dot_general x27, matrix products, contract_cells(): lax.dot_general(left, right, (((1,), (1,)), ((), ())), preferred_element_...  5.23 us
    ppermute x2, starting transfers between devices, extended(): lax.ppermute(head, axis, [((i + 1) % count, i) for i in range(ends)])  4.61 us
    ppermute x2, starting transfers between devices, extended(): lax.ppermute(tail, axis, [(i, (i + 1) % count) for i in range(ends)])  4.27 us
  transfers between devices with their start and end apart: 5, of which 3 were waited for; matrix products, arithmetic and copies ran while one was open for 23% of the time, Pallas kernels for 0%

profile of v1, /device:TPU:8, one launch (start us, length us, event | category | flops | bytes accessed | tf_op | source)
XLA Modules:
  0.0 148.7 jit_solution(11209371832599699137)
XLA Ops:
  8.1 1.7 %collective-permute-start = (bf16[32,1,4,128]{3,0,2,1:T(8,128)(2,1)S(1)}, bf16[32,1,4,128]{3,0,2,1:T(8,128)(2,1)S(1)}, u32[]{:S(2)}, u32[]{:S(2)}) collective-permute-start(bf16[32,1,4,128]{3,0,2,1:T(8,128)(2,1)S(1)} %copy.242), channel_id=1, source_target_pairs={{0,8},{8,16},{16,24},{1,9},{9,17},{17,25},{2,10},{10,18},{18,26},{... | collective-permute-start | bytes 98312 | tf_op jit(solution)/shard_map/ppermute | solution.py:15
  9.9 1.3 collective-permute-start.1
  11.2 1.0 constant_dynamic-update-slice_fusion.4
  12.2 2.0 %collective-permute-done.1 = bf16[32,1,4,128]{3,0,2,1:T(8,128)(2,1)S(1)} collective-permute-done((bf16[32,1,4,128]{3,0,2,1:T(8,128)(2,1)S(1)}, bf16[32,1,4,128]{3,0,2,1:T(8,128)(2,1)S(1)}, u32[]{:S(2)}, u32[]{:S(2)}) %collective-permute-start.1) | collective-permute-done | bytes 32800 | tf_op jit(solution)/shard_map/ppermute | solution.py:17
  14.3 3.3 %collective-permute-start.3 = (bf16[32,6,1,128]{3,0,2,1:T(8,128)(2,1)S(1)}, bf16[32,6,1,128]{3,0,2,1:T(8,128)(2,1)S(1)}, u32[]{:S(2)}, u32[]{:S(2)}) collective-permute-start(bf16[32,6,1,128]{3,0,2,1:T(8,128)(2,1)S(1)} %get-tuple-element.30), channel_id=1, source_target_pairs={{1,0},{2,1},{3,2},{4,3},{5,4},{6,5},{7,6},{9,8},{10,9},{11,10},{12... | collective-permute-start | bytes 147464 | tf_op jit(solution)/shard_map/ppermute | solution.py:17
  17.6 2.5 %collective-permute-start.2 = (bf16[32,6,1,128]{3,0,2,1:T(8,128)(2,1)S(1)}, bf16[32,6,1,128]{3,0,2,1:T(8,128)(2,1)S(1)}, u32[]{:S(2)}, u32[]{:S(2)}) collective-permute-start(bf16[32,6,1,128]{3,0,2,1:T(8,128)(2,1)S(1)} %get-tuple-element.29), channel_id=1, source_target_pairs={{0,1},{1,2},{2,3},{3,4},{4,5},{5,6},{6,7},{8,9},{9,10},{10,11},{11... | collective-permute-start | bytes 147464 | tf_op jit(solution)/shard_map/ppermute | solution.py:15
  21.9 2.6 %collective-permute-done.2 = bf16[32,6,1,128]{3,0,2,1:T(8,128)(2,1)S(1)} collective-permute-done((bf16[32,6,1,128]{3,0,2,1:T(8,128)(2,1)S(1)}, bf16[32,6,1,128]{3,0,2,1:T(8,128)(2,1)S(1)}, u32[]{:S(2)}, u32[]{:S(2)}) %collective-permute-start.2) | collective-permute-done | bytes 49184 | tf_op jit(solution)/shard_map/ppermute | solution.py:15
  30.8 0.9 convolution_bitcast_fusion.4
  31.8 1.2 fusion.161
  33.2 1.7 %fusion.52 = (bf16[32,4,4,128]{3,0,2,1:T(8,128)(2,1)S(1)}, bf16[32,4,4,128]{3,0,2,1:T(8,128)(2,1)S(1)}, bf16[32,4,4,128]{3,0,2,1:T(8,128)(2,1)}, bf16[32,4,4,128...) fusion(bf16[32,6,4,128]{3,0,2,1:T(8,128)(2,1)S(1)} %get-tuple-element.37, ...), kind=kLoop, calls=%fused_computation.122 | loop fusion | flops 393216 | bytes 1081344 | tf_op jit(solution)/shard_map/concatenate | solution.py:13
  36.2 1.0 reshape.108
  37.2 1.6 %copy.119 = bf16[32,4,4,128]{3,2,1,0:T(4,128)(2,1)} copy(bf16[32,4,4,128]{3,0,2,1:T(8,128)(2,1)} %get-tuple-element.22) | data formatting | bytes 262144 | tf_op jit(solution)/shard_map/slice | solution.py:45
  38.9 1.0 reshape.107
  40.6 1.0 reshape.106
  42.3 1.0 reshape.105
  44.0 1.0 reshape.104
  45.7 1.0 reshape.103
  47.4 1.0 reshape.88
  49.1 1.6 %reshape.89 = bf16[32,2048]{1,0:T(8,128)(2,1)} reshape(bf16[32,4,4,128]{3,2,1,0:T(4,128)(2,1)} %copy.101) | data formatting | bytes 262144 | tf_op jit(solution)/shard_map/reshape | solution.py:50
  53.1 1.0 convolution_bitcast_fusion
  54.1 0.9 convolution_bitcast_fusion.1
  55.1 0.9 convolution_bitcast_fusion.2
  62.2 72.1 %all-gather.2.cloned.1.call-done = f32[32,3,3,3,32,32]{5,4,3,2,1,0:T(8,128)} async-done(((f32[1,3,3,3,32,32]{5,4,3,2,1,0:T(8,128)}), f32[32,3,3,3,32,32]{5,4,3,2,1,0:T(8,128)}) %all-gather.2.cloned.1.call-update) | async-done | bytes 3538960 | tf_op jit(solution)/shard_map/all_gather | solution.py:57
  134.2 6.9 %reduce_sum.9 = f32[3,3,3,32,32]{4,3,2,1,0:T(8,128)S(1)} reduce(f32[32,3,3,3,32,32]{5,4,3,2,1,0:T(8,128)} %all-gather.2.cloned.1.call-done, f32[]{:T(128)} %constant.6.clone.1), dimensions={0}, to_apply=%region_0.1 | reduce | flops 857088 | bytes 3649540 | tf_op jit(solution)/shard_map/reduce_sum | solution.py:57
  (135 shorter events, 23.8 us)
Async XLA Ops:
  7.2 17.6 %copy-start = (bf16[32,4,4,128]{3,2,1,0:T(4,128)(2,1)S(1)}, bf16[32,4,4,128]{3,2,1,0:T(4,128)(2,1)}, u32[]{:S(2)}) copy-start(bf16[32,4,4,128]{3,2,1,0:T(4,128)(2,1)} %param.3) | copy-start | bytes 393220
  7.2 13.0 %copy-start.1 = (bf16[32,4,4,128]{3,2,1,0:T(4,128)(2,1)S(1)}, bf16[32,4,4,128]{3,2,1,0:T(4,128)(2,1)}, u32[]{:S(2)}) copy-start(bf16[32,4,4,128]{3,2,1,0:T(4,128)(2,1)} %param.4) | copy-start | bytes 393220
  7.2 127.1 %all-gather.2.cloned.1.call-start = ((), (), s32[]{:S(2)}) async-start(), calls=%async_computation | async-start | bytes 14598144 | tf_op jit(solution)/shard_map/all_gather | solution.py:57
  8.1 3.1 %collective-permute-start = (bf16[32,1,4,128]{3,0,2,1:T(8,128)(2,1)S(1)}, bf16[32,1,4,128]{3,0,2,1:T(8,128)(2,1)S(1)}, u32[]{:S(2)}, u32[]{:S(2)}) collective-permute-start(bf16[32,1,4,128]{3,0,2,1:T(8,128)(2,1)S(1)} %copy.242), channel_id=1, source_target_pairs={{0,8},{8,16},{16,24},{1,9},{9,17},{17,25},{2,10},{10,18},{18,26},{... | collective-permute-start | bytes 98312 | tf_op jit(solution)/shard_map/ppermute | solution.py:15
  9.9 4.4 %collective-permute-start.1 = (bf16[32,1,4,128]{3,0,2,1:T(8,128)(2,1)S(1)}, bf16[32,1,4,128]{3,0,2,1:T(8,128)(2,1)S(1)}, u32[]{:S(2)}, u32[]{:S(2)}) collective-permute-start(bf16[32,1,4,128]{3,0,2,1:T(8,128)(2,1)S(1)} %copy.243), channel_id=1, source_target_pairs={{8,0},{16,8},{24,16},{9,1},{17,9},{25,17},{10,2},{18,10},{26,18},{... | collective-permute-start | bytes 98312 | tf_op jit(solution)/shard_map/ppermute | solution.py:17
  14.3 7.6 %collective-permute-start.3 = (bf16[32,6,1,128]{3,0,2,1:T(8,128)(2,1)S(1)}, bf16[32,6,1,128]{3,0,2,1:T(8,128)(2,1)S(1)}, u32[]{:S(2)}, u32[]{:S(2)}) collective-permute-start(bf16[32,6,1,128]{3,0,2,1:T(8,128)(2,1)S(1)} %get-tuple-element.30), channel_id=1, source_target_pairs={{1,0},{2,1},{3,2},{4,3},{5,4},{6,5},{7,6},{9,8},{10,9},{11,10},{12... | collective-permute-start | bytes 147464 | tf_op jit(solution)/shard_map/ppermute | solution.py:17
  17.6 6.9 %collective-permute-start.2 = (bf16[32,6,1,128]{3,0,2,1:T(8,128)(2,1)S(1)}, bf16[32,6,1,128]{3,0,2,1:T(8,128)(2,1)S(1)}, u32[]{:S(2)}, u32[]{:S(2)}) collective-permute-start(bf16[32,6,1,128]{3,0,2,1:T(8,128)(2,1)S(1)} %get-tuple-element.29), channel_id=1, source_target_pairs={{0,1},{1,2},{2,3},{3,4},{4,5},{5,6},{6,7},{8,9},{9,10},{10,11},{11... | collective-permute-start | bytes 147464 | tf_op jit(solution)/shard_map/ppermute | solution.py:15
  21.9 6.7 %copy-start.11 = (bf16[32,6,1,128]{3,0,2,1:T(8,128)(2,1)}, bf16[32,6,1,128]{3,0,2,1:T(8,128)(2,1)S(1)}, u32[]{:S(2)}) copy-start(bf16[32,6,1,128]{3,0,2,1:T(8,128)(2,1)S(1)} %collective-permute-done.3) | copy-start | bytes 147460
  24.5 5.2 %copy-start.12 = (bf16[32,6,1,128]{3,0,2,1:T(8,128)(2,1)}, bf16[32,6,1,128]{3,0,2,1:T(8,128)(2,1)S(1)}, u32[]{:S(2)}) copy-start(bf16[32,6,1,128]{3,0,2,1:T(8,128)(2,1)S(1)} %collective-permute-done.2) | copy-start | bytes 147460
  30.0 0.8 copy-start.9
  33.0 2.0 %copy-start.4 = (bf16[32,4,4,128]{3,0,2,1:T(8,128)(2,1)S(1)}, bf16[32,4,4,128]{3,0,2,1:T(8,128)(2,1)}, u32[]{:S(2)}) copy-start(bf16[32,4,4,128]{3,0,2,1:T(8,128)(2,1)} %get-tuple-element.3) | copy-start | bytes 393220
  33.1 2.1 %copy-start.2 = (bf16[32,4,4,128]{3,0,2,1:T(8,128)(2,1)S(1)}, bf16[32,4,4,128]{3,0,2,1:T(8,128)(2,1)}, u32[]{:S(2)}) copy-start(bf16[32,4,4,128]{3,0,2,1:T(8,128)(2,1)} %get-tuple-element.4) | copy-start | bytes 393220
  35.4 7.8 %copy-start.3 = (bf16[32,4,4,128]{3,0,2,1:T(8,128)(2,1)S(1)}, bf16[32,4,4,128]{3,0,2,1:T(8,128)(2,1)}, u32[]{:S(2)}) copy-start(bf16[32,4,4,128]{3,0,2,1:T(8,128)(2,1)} %get-tuple-element.27) | copy-start | bytes 393220
  53.1 2.9 %copy-start.10 = (bf16[3,3,3,32,32]{4,3,2,1,0:T(8,128)(2,1)S(1)}, bf16[3,3,3,32,32]{4,3,2,1,0:T(8,128)(2,1)}, u32[]{:S(2)}) copy-start(bf16[3,3,3,32,32]{4,3,2,1,0:T(8,128)(2,1)} %param.5) | copy-start | bytes 165892
  56.7 1.4 copy-start.7
  57.1 1.2 copy-start.8
  57.8 0.9 copy-start.6
  59.9 0.9 copy-start.5
Sparse Core Ops, SparseCore 0:
  30.9 103.2 all-gather.1
